TPU v7x, 512 devices: a whole 4x8x8 slice. The times are simulated.
512 devices in a mesh: pitch: 32 (over x, z), span: 8 (over y), row: 2 (over core).
Axes of the slice: x: 4, y: 8, z: 8, core: 2. Of those that a mesh axis runs over, the one named last changes fastest.
Arguments:
- fields: float32 [3, 512, 128, 512], P(None, 'pitch', 'span', 'row'), may hold values from -6 to 6
- diffusivity: float32 [512, 128, 512], P('pitch', 'span', 'row'), may hold values from 0.01 to 0.1
- mean_flow: bfloat16 [128, 2, 512], P('span', None, 'row'), may hold values from -6 to 6
- radial_kernel: bfloat16 [128, 128], replicated
- tracer_values: float32 [10, 1048576], P(None, ('pitch', 'span', 'row')), may hold values from -6 to 6
- tracer_cells: int32 [1048576], P(('pitch', 'span', 'row')), may hold values from 0 to 65535
- tracer_dest: int32 [1048576, 1], P(('pitch', 'span', 'row')), may hold values from 0 to 31; in each aligned block of 2048 rows (0 to 2047, 2048 to 4095, ...) at most 128 rows name the same one
- interface_map: int32 [2, 512], P('row', 'pitch'), may hold values from 0 to 511, as said below
Outputs:
- advected: float32 [3, 512, 128, 512], P(None, 'pitch', 'span', 'row')
- arrived: float32 [10, 2097152], P(None, ('pitch', 'span', 'row'))
Inputs may be any that keep to these rules, and one draw needn't show every extreme that they name: `tracer_cells`: the local index of the owning cell within the block of the device that holds the tracer, i * 16 * 256 + r * 256 + a for local indices i, r, a. `tracer_dest`: at most 128 of the tracers of one device go to one pitch index. `interface_map`: for one offset o of each draw, row 0 holds (i + o) mod 512 and row 1 holds (i - o) mod 512, so the two rows are inverse permutations.
All inputs are finite; a program needn't handle non-finite values.
Results may differ from a plain program's by a relative error of at most 0.0015.
Values may be sent and summed in bfloat16 or wider, within the bound.
A program may use at most 128 MiB of HBM per device.

v0:
```python
import jax
import jax.numpy as jnp
from jax import lax
from jax.sharding import PartitionSpec as P

SUB = 2
TIME_STEP = 0.9
AXIAL_SPEED = 0.15
PITCH_SPEED = 0.15


def swapped(block, axis, apart):
    count = lax.axis_size(axis)
    route = []
    for low in range(count):
        high = low | 1 << apart
        if high != low and high < count:
            route += [(low, high), (high, low)]
    return lax.ppermute(block, axis, route)


def padded(cells, sides, width):
    for axis, dim in sides:
        count = lax.axis_size(axis)
        head = lax.slice_in_dim(cells, 0, width, axis=dim)
        tail = lax.slice_in_dim(cells, cells.shape[dim] - width, cells.shape[dim], axis=dim)
        cells = jnp.concatenate(
            [
                lax.ppermute(tail, axis, [(i, (i + 1) % count) for i in range(count)]),
                cells,
                lax.ppermute(head, axis, [((i + 1) % count, i) for i in range(count)]),
            ],
            axis=dim,
        )
    return cells


def face_flux(left_values, right_values, left_kappa, right_kappa, face_speed):
    diffusion = -0.5 * (left_kappa + right_kappa) * (right_values - left_values)
    if face_speed is None:
        return diffusion
    return (
        jnp.maximum(face_speed, 0.0) * left_values
        + jnp.minimum(face_speed, 0.0) * right_values
        + diffusion
    )


def interface_ghost(own_face, local_map):
    across = swapped(own_face, "row", 0)
    picked = lax.all_gather(across, "pitch", axis=1, tiled=True)
    return jnp.take(picked, local_map, axis=1)


def update_core(extended, speed_axial, speed_pitch, ghost_face, wall_mask, row_id):
    along_pitch = extended[:, :, 1:-1, :]
    pitch_flux = face_flux(
        along_pitch[:3, :-1],
        along_pitch[:3, 1:],
        along_pitch[3, :-1],
        along_pitch[3, 1:],
        speed_pitch,
    )
    along_radius = extended[:, 1:-1]
    radial_flux = (
        face_flux(
            along_radius[:3, :, :-1],
            along_radius[:3, :, 1:],
            along_radius[3, :, :-1],
            along_radius[3, :, 1:],
            None,
        )
        * wall_mask[:, None]
    )
    core = extended[:, 1:-1, 1:-1]
    pitch_cells = core.shape[1]
    full_stack = jnp.concatenate(
        [core, jnp.broadcast_to(speed_axial[None, None], (1, pitch_cells) + speed_axial.shape)], 0
    )
    upstream = jnp.where(row_id == 0, full_stack[..., 0], ghost_face)
    downstream = jnp.where(row_id == 0, ghost_face, full_stack[..., -1])
    line = jnp.concatenate([upstream[..., None], full_stack, downstream[..., None]], -1)
    face_speed = 0.5 * (line[4, ..., :-1] + line[4, ..., 1:])
    axial_flux = face_flux(
        line[:3, ..., :-1], line[:3, ..., 1:], line[3, ..., :-1], line[3, ..., 1:], face_speed
    )
    divergence = (
        pitch_flux[:, 1:]
        - pitch_flux[:, :-1]
        + radial_flux[:, :, 1:]
        - radial_flux[:, :, :-1]
        + axial_flux[..., 1:]
        - axial_flux[..., :-1]
    )
    return core[:3] - TIME_STEP * divergence


def advance(state, diffusivity, speed_axial, speed_pitch, local_map, wall_mask):
    pitch_cells = state.shape[1]
    stacked = jnp.concatenate([state, diffusivity[None]], 0)
    extended = padded(stacked, (("pitch", 1), ("span", 2)), 1)
    full_stack = jnp.concatenate(
        [stacked, jnp.broadcast_to(speed_axial[None, None], (1, pitch_cells) + speed_axial.shape)],
        0,
    )
    row_id = lax.axis_index("row")
    own_face = jnp.where(row_id == 0, full_stack[..., -1], full_stack[..., 0])
    ghost_face = interface_ghost(own_face, local_map)
    return update_core(extended, speed_axial, speed_pitch, ghost_face, wall_mask, row_id)


def local(
    fields,
    diffusivity,
    mean_flow,
    radial_kernel,
    tracer_values,
    tracer_cells,
    tracer_dest,
    interface_map,
):
    radial_cells = mean_flow.shape[0]
    axial_cells = mean_flow.shape[2]
    flat_width = 2 * axial_cells
    span_id = lax.axis_index("span")
    kernel_cols = lax.dynamic_slice_in_dim(radial_kernel, span_id * radial_cells, radial_cells, 1)
    flat_rows = mean_flow.reshape(radial_cells, flat_width)
    smoothed = lax.psum_scatter(
        jnp.dot(kernel_cols, flat_rows, preferred_element_type=jnp.float32),
        "span",
        scatter_dimension=0,
        tiled=True,
    )
    smoothed = smoothed.reshape(radial_cells, 2, axial_cells)
    speed_axial = AXIAL_SPEED * (1.0 + 0.5 * jnp.tanh(smoothed[:, 0]))
    speed_pitch = PITCH_SPEED * jnp.tanh(smoothed[:, 1])
    plane_size = radial_cells * axial_cells
    sample_fields = jnp.take(fields.reshape(fields.shape[0], -1), tracer_cells, axis=1)
    sample_speed = jnp.take(
        jnp.stack([speed_axial, speed_pitch]).reshape(2, plane_size),
        tracer_cells % plane_size,
        axis=1,
    )
    sampled = jnp.concatenate([sample_fields, sample_speed], 0)
    head_rows = tracer_values[:5]
    tail_rows = tracer_values[5:]
    updated = jnp.concatenate(
        [head_rows + 0.5 * (sampled - head_rows), tail_rows + 0.8 * sampled], 0
    )
    npitch = lax.axis_size("pitch")
    capacity = 2 * tracer_values.shape[1] // npitch
    targets = tracer_dest[:, 0]
    onehot = (targets[:, None] == jnp.arange(npitch, dtype=jnp.int32)[None]).astype(jnp.int32)
    slot_index = jnp.sum((jnp.cumsum(onehot, 0) - onehot) * onehot, 1)
    position = targets * capacity + slot_index
    outgoing = (
        jnp.zeros((tracer_values.shape[0], npitch * capacity), jnp.float32)
        .at[:, position]
        .set(updated)
    )
    arrived = lax.all_to_all(outgoing, "pitch", split_axis=1, concat_axis=1, tiled=True)
    face_index = span_id * radial_cells + jnp.arange(radial_cells + 1, dtype=jnp.int32)
    total_radial = radial_cells * lax.axis_size("span")
    wall_mask = ((face_index > 0) & (face_index < total_radial)).astype(jnp.float32)
    local_map = interface_map[0]
    current = fields
    for substep in range(SUB):
        current = advance(current, diffusivity, speed_axial, speed_pitch, local_map, wall_mask)
    return (current, arrived)


def solution(mesh):
    placed = (
        P(None, "pitch", "span", "row"),
        P("pitch", "span", "row"),
        P("span", None, "row"),
        P(),
        P(None, ("pitch", "span", "row")),
        P(("pitch", "span", "row")),
        P(("pitch", "span", "row"), None),
        P("row", "pitch"),
    )
    return jax.shard_map(
        local,
        mesh=mesh,
        in_specs=placed,
        out_specs=(P(None, "pitch", "span", "row"), P(None, ("pitch", "span", "row"))),
        check_vma=False,
    )
```

profile of v0, /device:TPU:24, one launch (start us, length us, event | category | flops | bytes accessed | tf_op | source)
XLA Modules:
  0.0 287.4 jit_solution(10924218289385498217)
XLA Ops:
  10.5 4.3 %collective-permute-start = (f32[4,1,16,256]{3,2,1,0:T(8,128)}, f32[4,1,16,256]{3,2,1,0:T(8,128)S(1)}, u32[]{:S(2)}, u32[]{:S(2)}) collective-permute-start(f32[4,1,16,256]{3,2,1,0:T(8,128)} %get-tuple-element.57), channel_id=1, source_target_pairs={{0,16},{16,32},{32,48},{48,64},{64,80},{80,96},{96,112},{112,128},... | collective-permute-start | bytes 196616 | tf_op jit(solution)/shard_map/ppermute | solution.py:29
  14.7 10.8 %collective-permute-start.1 = (f32[4,1,16,256]{3,2,1,0:T(8,128)}, f32[4,1,16,256]{3,2,1,0:T(8,128)}, u32[]{:S(2)}, u32[]{:S(2)}) collective-permute-start(f32[4,1,16,256]{3,2,1,0:T(8,128)} %get-tuple-element.58), channel_id=1, source_target_pairs={{16,0},{32,16},{48,32},{64,48},{80,64},{96,80},{112,96},{128,112},... | collective-permute-start | bytes 196616 | tf_op jit(solution)/shard_map/ppermute | solution.py:31
  27.7 16.7 %copy.818 = f32[3,16,16,256]{0,3,2,1:T(8,128)} copy(f32[3,16,16,256]{3,2,1,0:T(8,128)S(1)} %copy-done.2) | data formatting | bytes 1572864 | tf_op args[0]
  44.4 18.2 %gather_fusion = f32[2048,3]{1,0:T(8,128)} fusion(f32[3,65536]{0,1:T(8,128)} %bitcast.121, s32[2048]{0:T(1024)S(1)} %get-tuple-element.74), kind=kCustom, calls=%fused_computation.2 | custom fusion | bytes 57344 | tf_op jit(solution)/shard_map/jit(_take)/gather | solution.py:138
  62.6 2.6 select_bitcast_fusion.1
  65.2 2.2 copy.820
  67.3 9.1 %reduce-window.6 = s32[32,16,128]{2,1,0:T(8,128)S(1)} reduce-window(s32[32,16,128]{2,1,0:T(8,128)S(1)} %fusion.43, s32[]{:T(128)} %constant.30.clone.1), window={size=1x1x128 pad=0_0x0_0x127_0}, to_apply=%region_1.0 | reduce-window | flops 8323072 | bytes 524292 | tf_op jit(solution)/shard_map/reduce-window
  79.0 4.7 %collective-permute-start.2 = (f32[4,18,1,256]{3,0,2,1:T(4,128)S(1)}, f32[4,18,1,256]{3,0,2,1:T(4,128)S(1)}, u32[]{:S(2)}, u32[]{:S(2)}) collective-permute-start(f32[4,18,1,256]{3,0,2,1:T(4,128)S(1)} %copy.846), channel_id=1, source_target_pairs={{0,2},{2,4},{4,6},{6,8},{8,10},{10,12},{12,14},{14,0},{1,3},{3,5},... | collective-permute-start | bytes 221192 | tf_op jit(solution)/shard_map/ppermute | solution.py:29
  85.7 2.2 fusion.14
  98.8 7.6 %gather_fusion.1 = f32[2048,2]{1,0:T(8,128)} fusion(f32[2,4096]{0,1:T(8,128)S(1)} %copy.819, s32[2048]{0:T(1024)S(1)} %get-tuple-element.75), kind=kCustom, calls=%fused_computation.3 | custom fusion | bytes 40960 | tf_op jit(solution)/shard_map/jit(_take)/gather | solution.py:139
  109.8 6.5 %scatter_custom_fusion = f32[10,4096]{0,1:T(8,128)S(1)} fusion(s32[2048]{0:T(1024)} %bitcast.141, f32[2048,10]{1,0:T(8,128)} %copy.822, f32[]{:T(128)} %constant.45.clone.1), kind=kCustom, calls=%fused_computation.51 | custom fusion | bytes 164352 | tf_op jit(solution)/shard_map/scatter | solution.py:159
  117.6 5.2 %all-to-all-start = ((f32[10,32,128]{2,0,1:T(8,128)}), f32[10,32,128]{2,0,1:T(8,128)}, u32[]{:S(2)}, u32[]{:S(2)}) async-start(f32[10,32,128]{2,0,1:T(8,128)} %copy.823), calls=%async_computation.1 | async-start | bytes 524288 | tf_op jit(solution)/shard_map/all_to_all | solution.py:161
  122.8 2.5 fusion.5
  126.2 51.2 %all_gather.6 = f32[5,512,16]{2,1,0:T(8,128)S(1)} all-gather(f32[5,16,16]{2,1,0:T(8,128)S(1)} %copy.782), channel_id=1, replica_groups=mesh['pitch'=32,'span'=8,'row'=2] {'pitch'}, dimensions={1}, use_global_device_ids=true | all-gather | bytes 168960 | tf_op jit(solution)/shard_map/all_gather | solution.py:51
  177.3 2.2 copy.783
  179.5 2.8 gather_fusion.2
  183.9 2.2 copy.786
  198.8 2.7 collective-permute-start.5
  201.4 6.5 %collective-permute-start.6 = (f32[4,1,16,256]{3,2,1,0:T(8,128)S(1)}, f32[4,1,16,256]{3,2,1,0:T(8,128)S(1)}, u32[]{:S(2)}, u32[]{:S(2)}) collective-permute-start(f32[4,1,16,256]{3,2,1,0:T(8,128)S(1)} %get-tuple-element.54), channel_id=1, source_target_pairs={{16,0},{32,16},{48,32},{64,48},{80,64},{96,80},{112,96},{128,112},... | collective-permute-start | bytes 196616 | tf_op jit(solution)/shard_map/ppermute | solution.py:31
  208.0 47.9 %all_gather.7 = f32[5,512,16]{2,1,0:T(8,128)S(1)} all-gather(f32[5,16,16]{2,1,0:T(8,128)S(1)} %copy.807), channel_id=1, replica_groups=mesh['pitch'=32,'span'=8,'row'=2] {'pitch'}, dimensions={1}, use_global_device_ids=true | all-gather | bytes 168960 | tf_op jit(solution)/shard_map/all_gather | solution.py:51
  255.8 2.2 copy.808
  258.0 2.1 gather_fusion.3
  264.8 4.3 %collective-permute-start.7 = (f32[4,18,1,256]{3,0,2,1:T(4,128)S(1)}, f32[4,18,1,256]{3,0,2,1:T(4,128)S(1)}, u32[]{:S(2)}, u32[]{:S(2)}) collective-permute-start(f32[4,18,1,256]{3,0,2,1:T(4,128)S(1)} %copy.851), channel_id=1, source_target_pairs={{0,2},{2,4},{4,6},{6,8},{8,10},{10,12},{12,14},{14,0},{1,3},{3,5},... | collective-permute-start | bytes 221192 | tf_op jit(solution)/shard_map/ppermute | solution.py:29
  273.2 3.3 %collective-permute-done.8 = f32[4,18,1,256]{3,0,2,1:T(4,128)S(1)} collective-permute-done((f32[4,18,1,256]{3,0,2,1:T(4,128)S(1)}, f32[4,18,1,256]{3,0,2,1:T(4,128)S(1)}, u32[]{:S(2)}, u32[]{:S(2)}) %collective-permute-start.8) | collective-permute-done | bytes 73760 | tf_op jit(solution)/shard_map/ppermute | solution.py:31
  (142 shorter events, 52.9 us)
Async XLA Ops:
  7.2 18.4 %copy-start = (bf16[128,128]{1,0:T(8,128)(2,1)S(1)}, bf16[128,128]{1,0:T(8,128)(2,1)}, u32[]{:S(2)}) copy-start(bf16[128,128]{1,0:T(8,128)(2,1)} %param.13) | copy-start | bytes 98308
  7.2 85.3 %reduce-scatter.2.cloned.1.call-start = ((), (), s32[]{:S(2)}) async-start(), calls=%async_computation.2 | async-start | bytes 294912 | tf_op jit(solution)/shard_map/reduce_scatter | solution.py:128
  8.3 17.2 %copy-start.12 = (bf16[16,2,256]{2,1,0:T(2,128)(2,1)S(1)}, bf16[16,2,256]{2,1,0:T(2,128)(2,1)}, u32[]{:S(2)}) copy-start(bf16[16,2,256]{2,1,0:T(2,128)(2,1)} %param.12) | copy-start | bytes 49156
  8.3 18.2 %copy-start.2 = (f32[3,16,16,256]{3,2,1,0:T(8,128)S(1)}, f32[3,16,16,256]{3,2,1,0:T(8,128)}, u32[]{:S(2)}) copy-start(f32[3,16,16,256]{3,2,1,0:T(8,128)} %param.10) | copy-start | bytes 2359300
  9.8 17.2 %copy-start.16 = (s32[1,16]{1,0:T(1,128)S(1)}, s32[1,16]{1,0:T(1,128)}, u32[]{:S(2)}) copy-start(s32[1,16]{1,0:T(1,128)} %param.17) | copy-start | bytes 196
  9.8 17.9 %copy-start.11 = (s32[2048]{0:T(1024)S(1)}, s32[2048]{0:T(1024)}, u32[]{:S(2)}) copy-start(s32[2048]{0:T(1024)} %param.15) | copy-start | bytes 24580
  10.5 67.4 %collective-permute-start = (f32[4,1,16,256]{3,2,1,0:T(8,128)}, f32[4,1,16,256]{3,2,1,0:T(8,128)S(1)}, u32[]{:S(2)}, u32[]{:S(2)}) collective-permute-start(f32[4,1,16,256]{3,2,1,0:T(8,128)} %get-tuple-element.57), channel_id=1, source_target_pairs={{0,16},{16,32},{32,48},{48,64},{64,80},{80,96},{96,112},{112,128},... | collective-permute-start | bytes 196616 | tf_op jit(solution)/shard_map/ppermute | solution.py:29
  14.7 63.1 %collective-permute-start.1 = (f32[4,1,16,256]{3,2,1,0:T(8,128)}, f32[4,1,16,256]{3,2,1,0:T(8,128)}, u32[]{:S(2)}, u32[]{:S(2)}) collective-permute-start(f32[4,1,16,256]{3,2,1,0:T(8,128)} %get-tuple-element.58), channel_id=1, source_target_pairs={{16,0},{32,16},{48,32},{64,48},{80,64},{96,80},{112,96},{128,112},... | collective-permute-start | bytes 196616 | tf_op jit(solution)/shard_map/ppermute | solution.py:31
  27.0 66.3 %copy-start.3 = (f32[3,16,16,256]{3,1,2,0:T(8,128)}, f32[3,16,16,256]{3,1,2,0:T(8,128)S(1)}, u32[]{:S(2)}) copy-start(f32[3,16,16,256]{3,1,2,0:T(8,128)S(1)} %copy.791) | copy-start | bytes 2359300
  62.6 4.7 %copy-start.10 = (s32[2048,1]{0,1:T(1,128)S(1)}, s32[2048,1]{0,1:T(1,128)}, u32[]{:S(2)}) copy-start(s32[2048,1]{0,1:T(1,128)} %param.16) | copy-start | bytes 24580
  77.9 13.4 %copy-start.13 = (f32[17]{0:T(128)}, f32[17]{0:T(128)S(1)}, u32[]{:S(2)}) copy-start(f32[17]{0:T(128)S(1)} %and_convert_fusion) | copy-start | bytes 208
  79.0 10.6 %collective-permute-start.2 = (f32[4,18,1,256]{3,0,2,1:T(4,128)S(1)}, f32[4,18,1,256]{3,0,2,1:T(4,128)S(1)}, u32[]{:S(2)}, u32[]{:S(2)}) collective-permute-start(f32[4,18,1,256]{3,0,2,1:T(4,128)S(1)} %copy.846), channel_id=1, source_target_pairs={{0,2},{2,4},{4,6},{6,8},{8,10},{10,12},{12,14},{14,0},{1,3},{3,5},... | collective-permute-start | bytes 221192 | tf_op jit(solution)/shard_map/ppermute | solution.py:29
  83.7 7.5 %collective-permute-start.3 = (f32[4,18,1,256]{3,0,2,1:T(4,128)S(1)}, f32[4,18,1,256]{3,0,2,1:T(4,128)S(1)}, u32[]{:S(2)}, u32[]{:S(2)}) collective-permute-start(f32[4,18,1,256]{3,0,2,1:T(4,128)S(1)} %copy.847), channel_id=1, source_target_pairs={{2,0},{4,2},{6,4},{8,6},{10,8},{12,10},{14,12},{0,14},{3,1},{5,3},... | collective-permute-start | bytes 221192 | tf_op jit(solution)/shard_map/ppermute | solution.py:31
  96.1 29.2 %collective-permute-start.4 = (f32[5,16,16]{2,0,1:T(8,128)}, f32[5,16,16]{2,0,1:T(8,128)}, u32[]{:S(2)}, u32[]{:S(2)}) collective-permute-start(f32[5,16,16]{2,0,1:T(8,128)} %bitcast_select_fusion.5), channel_id=1, source_target_pairs={{0,1},{1,0},{2,3},{3,2},{4,5},{5,4},{6,7},{7,6},{8,9},{9,8},{10,11... | collective-permute-start | bytes 15368 | tf_op jit(solution)/shard_map/ppermute | solution.py:19
  117.6 161.1 %all-to-all-start = ((f32[10,32,128]{2,0,1:T(8,128)}), f32[10,32,128]{2,0,1:T(8,128)}, u32[]{:S(2)}, u32[]{:S(2)}) async-start(f32[10,32,128]{2,0,1:T(8,128)} %copy.823), calls=%async_computation.1 | async-start | bytes 524288 | tf_op jit(solution)/shard_map/all_to_all | solution.py:161
  177.3 5.0 %copy-start.7 = (f32[5,16,16,1]{2,0,1,3:T(8,128)S(1)}, f32[5,16,16,1]{2,0,1,3:T(8,128)}, u32[]{:S(2)}) copy-start(f32[5,16,16,1]{2,0,1,3:T(8,128)} %copy-done.6) | copy-start | bytes 15364
  177.3 5.0 %copy-start.15 = (pred[16]{0:T(512)(128)(4,1)S(1)}, pred[16]{0:T(512)(128)(4,1)}, u32[]{:S(2)}) copy-start(pred[16]{0:T(512)(128)(4,1)} %compare_and_fusion.2) | copy-start | bytes 52
  179.5 8.0 %copy-start.4 = (f32[3,16,16,256]{3,1,2,0:T(8,128)S(1)}, f32[3,16,16,256]{3,1,2,0:T(8,128)}, u32[]{:S(2)}) copy-start(f32[3,16,16,256]{3,1,2,0:T(8,128)} %copy-done.3) | copy-start | bytes 2359300
  196.2 11.7 %collective-permute-start.9 = (f32[5,16,16]{2,0,1:T(8,128)S(1)}, f32[5,16,16]{2,0,1:T(8,128)S(1)}, u32[]{:S(2)}, u32[]{:S(2)}) collective-permute-start(f32[5,16,16]{2,0,1:T(8,128)S(1)} %bitcast_select_fusion.2), channel_id=1, source_target_pairs={{0,1},{1,0},{2,3},{3,2},{4,5},{5,4},{6,7},{7,6},{8,9},{9,8},{10,11... | collective-permute-start | bytes 15368 | tf_op jit(solution)/shard_map/ppermute | solution.py:19
  198.8 65.5 %collective-permute-start.5 = (f32[4,1,16,256]{3,2,1,0:T(8,128)}, f32[4,1,16,256]{3,2,1,0:T(8,128)S(1)}, u32[]{:S(2)}, u32[]{:S(2)}) collective-permute-start(f32[4,1,16,256]{3,2,1,0:T(8,128)} %get-tuple-element.53), channel_id=1, source_target_pairs={{0,16},{16,32},{32,48},{48,64},{64,80},{80,96},{96,112},{112,128},... | collective-permute-start | bytes 196616 | tf_op jit(solution)/shard_map/ppermute | solution.py:29
  201.4 62.9 %collective-permute-start.6 = (f32[4,1,16,256]{3,2,1,0:T(8,128)S(1)}, f32[4,1,16,256]{3,2,1,0:T(8,128)S(1)}, u32[]{:S(2)}, u32[]{:S(2)}) collective-permute-start(f32[4,1,16,256]{3,2,1,0:T(8,128)S(1)} %get-tuple-element.54), channel_id=1, source_target_pairs={{16,0},{32,16},{48,32},{64,48},{80,64},{96,80},{112,96},{128,112},... | collective-permute-start | bytes 196616 | tf_op jit(solution)/shard_map/ppermute | solution.py:31
  264.8 7.7 %collective-permute-start.7 = (f32[4,18,1,256]{3,0,2,1:T(4,128)S(1)}, f32[4,18,1,256]{3,0,2,1:T(4,128)S(1)}, u32[]{:S(2)}, u32[]{:S(2)}) collective-permute-start(f32[4,18,1,256]{3,0,2,1:T(4,128)S(1)} %copy.851), channel_id=1, source_target_pairs={{0,2},{2,4},{4,6},{6,8},{8,10},{10,12},{12,14},{14,0},{1,3},{3,5},... | collective-permute-start | bytes 221192 | tf_op jit(solution)/shard_map/ppermute | solution.py:29
  269.0 7.5 %collective-permute-start.8 = (f32[4,18,1,256]{3,0,2,1:T(4,128)S(1)}, f32[4,18,1,256]{3,0,2,1:T(4,128)S(1)}, u32[]{:S(2)}, u32[]{:S(2)}) collective-permute-start(f32[4,18,1,256]{3,0,2,1:T(4,128)S(1)} %copy.852), channel_id=1, source_target_pairs={{2,0},{4,2},{6,4},{8,6},{10,8},{12,10},{14,12},{0,14},{3,1},{5,3},... | collective-permute-start | bytes 221192 | tf_op jit(solution)/shard_map/ppermute | solution.py:31
  272.4 4.2 %copy-start.14 = (f32[17]{0:T(128)S(1)}, f32[17]{0:T(128)}, u32[]{:S(2)}) copy-start(f32[17]{0:T(128)} %copy-done.13) | copy-start | bytes 208
  (5 other events, 11.4 us)
Sparse Core Ops, SparseCore 0:
  26.7 35.2 reduce-scatter.1
where the time goes:
time: 289 us; the launch traced here: 287 us
  blocking collectives  99 us (34%)
  local copies, waits for them, and re-layouts  89.4 us (31%)
  starting transfers between devices  46.3 us (16%)
  other arithmetic  32.7 us (11%)
  between operations  14.8 us (5%)
  waiting for transfers between devices  4.27 us (1%)
    all_gather x2, blocking collectives, interface_ghost(): picked = lax.all_gather(across, 'pitch', axis=1, tiled=True)  99 us
    unnamed x53, local copies, waits for them, and re-layouts  24.7 us
    ppermute x4, starting transfers between devices, padded(): lax.ppermute(head, axis, [((i + 1) % count, i) for i in range(count)])  21.3 us
    gather x1, local copies, waits for them, and re-layouts, local(): jnp.take(fields.reshape(fields.shape[0], -1), tracer_cells, axis=1)  18.2 us
    ppermute x4, starting transfers between devices, padded(): lax.ppermute(tail, axis, [(i, (i + 1) % count) for i in range(count)])  15.9 us
    another operation x3, other arithmetic  9.41 us
    gather x1, local copies, waits for them, and re-layouts, local(): jnp.take(jnp.stack([speed_axial, speed_pitch]).reshape(2, plane_size), tr...  7.6 us
    scatter x1, local copies, waits for them, and re-layouts, local(): outgoing = jnp.zeros((tracer_values.shape[0], npitch * capacity), jnp.flo...  6.46 us
  transfers between devices with their start and end apart: 12, of which 2 were waited for; matrix products, arithmetic and copies ran while one was open for 39% of the time, Pallas kernels for 0%

commit v1 on v0

--- a/solution.py
+++ b/solution.py
@@ -48,7 +48,9 @@
 
 def interface_ghost(own_face, local_map):
     across = swapped(own_face, "row", 0)
-    picked = lax.all_gather(across, "pitch", axis=1, tiled=True)
+    picked = jnp.concatenate(
+        lax.all_to_all(jnp.stack([across] * lax.axis_size("pitch")), "pitch", 0, 0), axis=1
+    )
     return jnp.take(picked, local_map, axis=1)
 
 

time: 289 us -> 241 us (0.83)
  the two profiles are of different devices: /device:TPU:24 before, /device:TPU:30 now
where the time goes in v1:
time: 241 us; the launch traced here: 239 us
  local copies, waits for them, and re-layouts  113 us (47%)
  starting transfers between devices  59 us (24%)
  other arithmetic  40.4 us (17%)
  between operations  14.8 us (6%)
  waiting for transfers between devices  10.6 us (4%)
    unnamed x61, local copies, waits for them, and re-layouts  37.6 us
    gather x1, local copies, waits for them, and re-layouts, local(): jnp.take(fields.reshape(fields.shape[0], -1), tracer_cells, axis=1)  18.2 us
    ppermute x4, starting transfers between devices, padded(): lax.ppermute(head, axis, [((i + 1) % count, i) for i in range(count)])  17.5 us
    ppermute x4, starting transfers between devices, padded(): lax.ppermute(tail, axis, [(i, (i + 1) % count) for i in range(count)])  17.2 us
    all_to_all x2, starting transfers between devices, interface_ghost(): lax.all_to_all(jnp.stack([across] * lax.axis_size('pitch')), 'pitch', 0, 0)  13.1 us
    reshape x4, local copies, waits for them, and re-layouts, interface_ghost(): jnp.concatenate(lax.all_to_all(jnp.stack([across] * lax.axis_size('pitch'...  10.5 us
    another operation x3, other arithmetic  9.41 us
    gather x1, local copies, waits for them, and re-layouts, local(): jnp.take(jnp.stack([speed_axial, speed_pitch]).reshape(2, plane_size), tr...  9.14 us
  transfers between devices with their start and end apart: 14, of which 4 were waited for; matrix products, arithmetic and copies ran while one was open for 44% of the time, Pallas kernels for 0%

profile of v1, /device:TPU:30, one launch (start us, length us, event | category | flops | bytes accessed | tf_op | source)
XLA Modules:
  0.0 239.0 jit_solution(7663790292442162014)
XLA Ops:
  10.5 4.3 %collective-permute-start = (f32[4,1,16,256]{3,2,1,0:T(8,128)}, f32[4,1,16,256]{3,2,1,0:T(8,128)S(1)}, u32[]{:S(2)}, u32[]{:S(2)}) collective-permute-start(f32[4,1,16,256]{3,2,1,0:T(8,128)} %get-tuple-element.57), channel_id=1, source_target_pairs={{0,16},{16,32},{32,48},{48,64},{64,80},{80,96},{96,112},{112,128},... | collective-permute-start | bytes 196616 | tf_op jit(solution)/shard_map/ppermute | solution.py:29
  14.7 8.9 %collective-permute-start.1 = (f32[4,1,16,256]{3,2,1,0:T(8,128)}, f32[4,1,16,256]{3,2,1,0:T(8,128)}, u32[]{:S(2)}, u32[]{:S(2)}) collective-permute-start(f32[4,1,16,256]{3,2,1,0:T(8,128)} %get-tuple-element.58), channel_id=1, source_target_pairs={{16,0},{32,16},{48,32},{64,48},{80,64},{96,80},{112,96},{128,112},... | collective-permute-start | bytes 196616 | tf_op jit(solution)/shard_map/ppermute | solution.py:31
  26.9 16.6 %copy.838 = f32[3,16,16,256]{0,3,2,1:T(8,128)} copy(f32[3,16,16,256]{3,2,1,0:T(8,128)S(1)} %copy-done.2) | data formatting | bytes 1572864 | tf_op args[0]
  44.1 18.2 %gather_fusion = f32[2048,3]{1,0:T(8,128)} fusion(f32[3,65536]{0,1:T(8,128)} %bitcast.135, s32[2048]{0:T(1024)S(1)} %get-tuple-element.74), kind=kCustom, calls=%fused_computation.2 | custom fusion | bytes 57344 | tf_op jit(solution)/shard_map/jit(_take)/gather | solution.py:140
  62.3 2.6 %select_bitcast_fusion.1 = f32[3,2048]{0,1:T(8,128)} fusion(f32[2048,3]{1,0:T(8,128)} %gather_fusion, pred[2048]{0:T(1024)(128)(4,1)S(1)} %get-tuple-element.72), kind=kLoop, calls=%fused_computation.50 | loop fusion | flops 6144 | bytes 51200 | tf_op jit(solution)/shard_map/jit(_take)/select_n | solution.py:140
  66.4 9.1 %reduce-window.6 = s32[32,16,128]{2,1,0:T(8,128)S(1)} reduce-window(s32[32,16,128]{2,1,0:T(8,128)S(1)} %fusion.43, s32[]{:T(128)} %constant.30.clone.1), window={size=1x1x128 pad=0_0x0_0x127_0}, to_apply=%region_1.0 | reduce-window | flops 8323072 | bytes 524292 | tf_op jit(solution)/shard_map/reduce-window
  78.6 4.7 %collective-permute-start.2 = (f32[4,18,1,256]{3,0,2,1:T(4,128)S(1)}, f32[4,18,1,256]{3,0,2,1:T(4,128)S(1)}, u32[]{:S(2)}, u32[]{:S(2)}) collective-permute-start(f32[4,18,1,256]{3,0,2,1:T(4,128)S(1)} %copy.870), channel_id=1, source_target_pairs={{0,2},{2,4},{4,6},{6,8},{8,10},{10,12},{12,14},{14,0},{1,3},{3,5},... | collective-permute-start | bytes 221192 | tf_op jit(solution)/shard_map/ppermute | solution.py:29
  101.7 9.1 %gather_fusion.1 = f32[2048,2]{1,0:T(8,128)} fusion(f32[2,4096]{0,1:T(8,128)} %copy.839, s32[2048]{0:T(1024)S(1)} %copy-done.12), kind=kCustom, calls=%fused_computation.3 | custom fusion | bytes 40960 | tf_op jit(solution)/shard_map/jit(_take)/gather | solution.py:141
  116.2 7.2 %scatter_custom_fusion = f32[10,4096]{0,1:T(8,128)} fusion(s32[2048]{0:T(1024)} %bitcast.157, f32[2048,10]{1,0:T(8,128)S(1)} %copy.842, f32[]{:T(128)} %constant.45.clone.1), kind=kCustom, calls=%fused_computation.51 | custom fusion | bytes 164352 | tf_op jit(solution)/shard_map/scatter | solution.py:161
  123.4 2.9 %copy.843 = f32[10,32,128]{2,0,1:T(8,128)} copy(f32[10,32,128]{0,2,1:T(8,128)} %bitcast.142) | data formatting | bytes 327680 | tf_op jit(solution)/shard_map/all_to_all | solution.py:163
  126.3 7.4 %all-to-all-start.2 = ((f32[10,32,128]{2,0,1:T(8,128)}), f32[10,32,128]{2,0,1:T(8,128)}, u32[]{:S(2)}, u32[]{:S(2)}) async-start(f32[10,32,128]{2,0,1:T(8,128)} %copy.843), calls=%async_computation.3 | async-start | bytes 524288 | tf_op jit(solution)/shard_map/all_to_all | solution.py:163
  133.7 2.9 %fusion.19 = f32[3,16,17,256]{3,1,2,0:T(8,128)} fusion(f32[4,18,17,256]{3,1,2,0:T(8,128)} %copy-done.8, f32[4,18,17,256]{3,1,2,0:T(8,128)} %copy-done.6, f32[17]{0:T(128)S(1)} %copy-done.16, f32[16,17,256]{2,0,1:T(8,128)S(1)} %fusion.36), kind=kLoop, calls=%fused_computation.62 | loop fusion | flops 626688 | bytes 2785348 | tf_op jit(solution)/shard_map/mul | solution.py:68
  138.6 2.5 %reshape.211 = f32[32,1,1280]{2,1,0:T(1,128)} reshape(f32[32,5,16,16]{3,2,1,0:T(8,128)} %broadcast_bitcast_fusion.1) | data formatting | bytes 327680
  141.1 4.0 %all-to-all-done.2 = f32[10,32,128]{2,0,1:T(8,128)} async-done(((f32[10,32,128]{2,0,1:T(8,128)}), f32[10,32,128]{2,0,1:T(8,128)}, u32[]{:S(2)}, u32[]{:S(2)}) %all-to-all-start.2) | async-done | bytes 163872 | tf_op jit(solution)/shard_map/all_to_all | solution.py:163
  145.1 6.2 %all-to-all-start = ((f32[32,1,1280]{2,1,0:T(1,128)}), f32[32,1,1280]{2,1,0:T(1,128)S(1)}, u32[]{:S(2)}, u32[]{:S(2)}) async-start(f32[32,1,1280]{2,1,0:T(1,128)} %reshape.211), calls=%async_computation.1 | async-start | bytes 327680 | tf_op jit(solution)/shard_map/all_to_all | solution.py:52
  151.3 3.3 %fusion.5 = f32[3,17,16,256]{3,1,2,0:T(8,128)} fusion(f32[3,17,16,256]{3,2,1,0:T(8,128)} %get-tuple-element.56, f32[3,17,16,256]{3,2,1,0:T(8,128)S(1)} %copy-done.7, f32[17,16,256]{2,0,1:T(8,128)} %copy.787, f32[16,256]{1,0:T(8,128)S(1)} %get-tuple-element.70, f32[16,256]{1,0:T(8,128)S(1)} %get-tuple-element.71), kind=kLoop, calls=%fused_computation.32 | loop fusion | flops 1253376 | bytes 2818048 | tf_op jit(solution)/shard_map/add | solution.py:43
  156.4 3.4 %all-to-all-done = f32[32,1,1280]{2,1,0:T(1,128)S(1)} async-done(((f32[32,1,1280]{2,1,0:T(1,128)}), f32[32,1,1280]{2,1,0:T(1,128)S(1)}, u32[]{:S(2)}, u32[]{:S(2)}) %all-to-all-start) | async-done | bytes 163872 | tf_op jit(solution)/shard_map/all_to_all | solution.py:52
  165.4 2.8 %copy.849 = f32[5,32,16,16]{3,0,2,1:T(8,128)} copy(f32[5,32,16,16]{2,3,0,1:T(8,128)} %bitcast_bitcast_fusion.2) | data formatting | bytes 327680 | tf_op jit(solution)/shard_map/reshape | solution.py:51
  183.3 3.4 %collective-permute-start.5 = (f32[4,1,16,256]{3,2,1,0:T(8,128)S(1)}, f32[4,1,16,256]{3,2,1,0:T(8,128)S(1)}, u32[]{:S(2)}, u32[]{:S(2)}) collective-permute-start(f32[4,1,16,256]{3,2,1,0:T(8,128)S(1)} %get-tuple-element.53), channel_id=1, source_target_pairs={{0,16},{16,32},{32,48},{48,64},{64,80},{80,96},{96,112},{112,128},... | collective-permute-start | bytes 196616 | tf_op jit(solution)/shard_map/ppermute | solution.py:29
  186.7 4.6 %collective-permute-start.6 = (f32[4,1,16,256]{3,2,1,0:T(8,128)S(1)}, f32[4,1,16,256]{3,2,1,0:T(8,128)S(1)}, u32[]{:S(2)}, u32[]{:S(2)}) collective-permute-start(f32[4,1,16,256]{3,2,1,0:T(8,128)S(1)} %get-tuple-element.54), channel_id=1, source_target_pairs={{16,0},{32,16},{48,32},{64,48},{80,64},{96,80},{112,96},{128,112},... | collective-permute-start | bytes 196616 | tf_op jit(solution)/shard_map/ppermute | solution.py:31
  192.5 2.5 %reshape.213 = f32[32,1,1280]{2,1,0:T(1,128)} reshape(f32[32,5,16,16]{3,2,1,0:T(8,128)} %broadcast_bitcast_fusion) | data formatting | bytes 327680
  195.0 7.0 %all-to-all-start.1 = ((f32[32,1,1280]{2,1,0:T(1,128)}), f32[32,1,1280]{2,1,0:T(1,128)S(1)}, u32[]{:S(2)}, u32[]{:S(2)}) async-start(f32[32,1,1280]{2,1,0:T(1,128)} %reshape.213), calls=%async_computation.2 | async-start | bytes 327680 | tf_op jit(solution)/shard_map/all_to_all | solution.py:52
  202.4 4.8 %collective-permute-start.7 = (f32[4,18,1,256]{3,0,2,1:T(4,128)S(1)}, f32[4,18,1,256]{3,0,2,1:T(4,128)S(1)}, u32[]{:S(2)}, u32[]{:S(2)}) collective-permute-start(f32[4,18,1,256]{3,0,2,1:T(4,128)S(1)} %copy.875), channel_id=1, source_target_pairs={{0,2},{2,4},{4,6},{6,8},{8,10},{10,12},{12,14},{14,0},{1,3},{3,5},... | collective-permute-start | bytes 221192 | tf_op jit(solution)/shard_map/ppermute | solution.py:29
  220.1 2.8 %copy.858 = f32[5,32,16,16]{3,0,2,1:T(8,128)} copy(f32[5,32,16,16]{2,3,0,1:T(8,128)} %bitcast_bitcast_fusion.1) | data formatting | bytes 327680 | tf_op jit(solution)/shard_map/reshape | solution.py:51
  (157 shorter events, 83.5 us)
Async XLA Ops:
  7.2 16.5 %copy-start = (bf16[128,128]{1,0:T(8,128)(2,1)S(1)}, bf16[128,128]{1,0:T(8,128)(2,1)}, u32[]{:S(2)}) copy-start(bf16[128,128]{1,0:T(8,128)(2,1)} %param.13) | copy-start | bytes 98308
  7.2 85.0 %reduce-scatter.2.cloned.1.call-start = ((), (), s32[]{:S(2)}) async-start(), calls=%async_computation.4 | async-start | bytes 294912 | tf_op jit(solution)/shard_map/reduce_scatter | solution.py:130
  8.3 15.3 %copy-start.14 = (bf16[16,2,256]{2,1,0:T(2,128)(2,1)S(1)}, bf16[16,2,256]{2,1,0:T(2,128)(2,1)}, u32[]{:S(2)}) copy-start(bf16[16,2,256]{2,1,0:T(2,128)(2,1)} %param.12) | copy-start | bytes 49156
  8.3 16.3 %copy-start.2 = (f32[3,16,16,256]{3,2,1,0:T(8,128)S(1)}, f32[3,16,16,256]{3,2,1,0:T(8,128)}, u32[]{:S(2)}) copy-start(f32[3,16,16,256]{3,2,1,0:T(8,128)} %param.10) | copy-start | bytes 2359300
  9.8 15.3 %copy-start.17 = (s32[1,16]{1,0:T(1,128)S(1)}, s32[1,16]{1,0:T(1,128)}, u32[]{:S(2)}) copy-start(s32[1,16]{1,0:T(1,128)} %param.17) | copy-start | bytes 196
  9.8 15.9 %copy-start.13 = (s32[2048]{0:T(1024)S(1)}, s32[2048]{0:T(1024)}, u32[]{:S(2)}) copy-start(s32[2048]{0:T(1024)} %param.15) | copy-start | bytes 24580
  10.5 67.1 %collective-permute-start = (f32[4,1,16,256]{3,2,1,0:T(8,128)}, f32[4,1,16,256]{3,2,1,0:T(8,128)S(1)}, u32[]{:S(2)}, u32[]{:S(2)}) collective-permute-start(f32[4,1,16,256]{3,2,1,0:T(8,128)} %get-tuple-element.57), channel_id=1, source_target_pairs={{0,16},{16,32},{32,48},{48,64},{64,80},{80,96},{96,112},{112,128},... | collective-permute-start | bytes 196616 | tf_op jit(solution)/shard_map/ppermute | solution.py:29
  14.7 62.8 %collective-permute-start.1 = (f32[4,1,16,256]{3,2,1,0:T(8,128)}, f32[4,1,16,256]{3,2,1,0:T(8,128)}, u32[]{:S(2)}, u32[]{:S(2)}) collective-permute-start(f32[4,1,16,256]{3,2,1,0:T(8,128)} %get-tuple-element.58), channel_id=1, source_target_pairs={{16,0},{32,16},{48,32},{64,48},{80,64},{96,80},{112,96},{128,112},... | collective-permute-start | bytes 196616 | tf_op jit(solution)/shard_map/ppermute | solution.py:31
  78.6 10.6 %collective-permute-start.2 = (f32[4,18,1,256]{3,0,2,1:T(4,128)S(1)}, f32[4,18,1,256]{3,0,2,1:T(4,128)S(1)}, u32[]{:S(2)}, u32[]{:S(2)}) collective-permute-start(f32[4,18,1,256]{3,0,2,1:T(4,128)S(1)} %copy.870), channel_id=1, source_target_pairs={{0,2},{2,4},{4,6},{6,8},{8,10},{10,12},{12,14},{14,0},{1,3},{3,5},... | collective-permute-start | bytes 221192 | tf_op jit(solution)/shard_map/ppermute | solution.py:29
  83.4 7.5 %collective-permute-start.3 = (f32[4,18,1,256]{3,0,2,1:T(4,128)S(1)}, f32[4,18,1,256]{3,0,2,1:T(4,128)S(1)}, u32[]{:S(2)}, u32[]{:S(2)}) collective-permute-start(f32[4,18,1,256]{3,0,2,1:T(4,128)S(1)} %copy.871), channel_id=1, source_target_pairs={{2,0},{4,2},{6,4},{8,6},{10,8},{12,10},{14,12},{0,14},{3,1},{5,3},... | collective-permute-start | bytes 221192 | tf_op jit(solution)/shard_map/ppermute | solution.py:31
  97.0 13.8 %copy-start.9 = (f32[5,16,16,1]{2,0,1,3:T(8,128)}, f32[5,16,16,1]{2,0,1,3:T(8,128)S(1)}, u32[]{:S(2)}) copy-start(f32[5,16,16,1]{2,0,1,3:T(8,128)S(1)} %copy.847) | copy-start | bytes 15364
  97.6 38.9 %collective-permute-start.4 = (f32[5,16,16]{2,0,1:T(8,128)}, f32[5,16,16]{2,0,1:T(8,128)}, u32[]{:S(2)}, u32[]{:S(2)}) collective-permute-start(f32[5,16,16]{2,0,1:T(8,128)} %bitcast_select_fusion.5), channel_id=1, source_target_pairs={{0,1},{1,0},{2,3},{3,2},{4,5},{5,4},{6,7},{7,6},{8,9},{9,8},{10,11... | collective-permute-start | bytes 15368 | tf_op jit(solution)/shard_map/ppermute | solution.py:19
  123.4 10.3 %copy-start.16 = (f32[17]{0:T(128)S(1)}, f32[17]{0:T(128)}, u32[]{:S(2)}) copy-start(f32[17]{0:T(128)} %and_convert_fusion) | copy-start | bytes 208
  126.3 18.8 %all-to-all-start.2 = ((f32[10,32,128]{2,0,1:T(8,128)}), f32[10,32,128]{2,0,1:T(8,128)}, u32[]{:S(2)}, u32[]{:S(2)}) async-start(f32[10,32,128]{2,0,1:T(8,128)} %copy.843), calls=%async_computation.3 | async-start | bytes 524288 | tf_op jit(solution)/shard_map/all_to_all | solution.py:163
  137.5 13.8 %copy-start.7 = (f32[3,17,16,256]{3,2,1,0:T(8,128)S(1)}, f32[3,17,16,256]{3,2,1,0:T(8,128)}, u32[]{:S(2)}) copy-start(f32[3,17,16,256]{3,2,1,0:T(8,128)} %get-tuple-element.55) | copy-start | bytes 2506756
  145.1 14.7 %all-to-all-start = ((f32[32,1,1280]{2,1,0:T(1,128)}), f32[32,1,1280]{2,1,0:T(1,128)S(1)}, u32[]{:S(2)}, u32[]{:S(2)}) async-start(f32[32,1,1280]{2,1,0:T(1,128)} %reshape.211), calls=%async_computation.1 | async-start | bytes 327680 | tf_op jit(solution)/shard_map/all_to_all | solution.py:52
  165.4 5.1 %copy-start.10 = (f32[5,16,16,1]{2,0,1,3:T(8,128)S(1)}, f32[5,16,16,1]{2,0,1,3:T(8,128)}, u32[]{:S(2)}) copy-start(f32[5,16,16,1]{2,0,1,3:T(8,128)} %copy-done.9) | copy-start | bytes 15364
  165.4 5.1 %copy-start.15 = (pred[16]{0:T(512)(128)(4,1)S(1)}, pred[16]{0:T(512)(128)(4,1)}, u32[]{:S(2)}) copy-start(pred[16]{0:T(512)(128)(4,1)} %compare_and_fusion.2) | copy-start | bytes 52
  181.3 9.9 %collective-permute-start.9 = (f32[5,16,16]{2,0,1:T(8,128)S(1)}, f32[5,16,16]{2,0,1:T(8,128)S(1)}, u32[]{:S(2)}, u32[]{:S(2)}) collective-permute-start(f32[5,16,16]{2,0,1:T(8,128)S(1)} %bitcast_select_fusion.2), channel_id=1, source_target_pairs={{0,1},{1,0},{2,3},{3,2},{4,5},{5,4},{6,7},{7,6},{8,9},{9,8},{10,11... | collective-permute-start | bytes 15368 | tf_op jit(solution)/shard_map/ppermute | solution.py:19
  183.3 18.7 %collective-permute-start.5 = (f32[4,1,16,256]{3,2,1,0:T(8,128)S(1)}, f32[4,1,16,256]{3,2,1,0:T(8,128)S(1)}, u32[]{:S(2)}, u32[]{:S(2)}) collective-permute-start(f32[4,1,16,256]{3,2,1,0:T(8,128)S(1)} %get-tuple-element.53), channel_id=1, source_target_pairs={{0,16},{16,32},{32,48},{48,64},{64,80},{80,96},{96,112},{112,128},... | collective-permute-start | bytes 196616 | tf_op jit(solution)/shard_map/ppermute | solution.py:29
  186.7 15.3 %collective-permute-start.6 = (f32[4,1,16,256]{3,2,1,0:T(8,128)S(1)}, f32[4,1,16,256]{3,2,1,0:T(8,128)S(1)}, u32[]{:S(2)}, u32[]{:S(2)}) collective-permute-start(f32[4,1,16,256]{3,2,1,0:T(8,128)S(1)} %get-tuple-element.54), channel_id=1, source_target_pairs={{16,0},{32,16},{48,32},{64,48},{80,64},{96,80},{112,96},{128,112},... | collective-permute-start | bytes 196616 | tf_op jit(solution)/shard_map/ppermute | solution.py:31
  195.0 20.1 %all-to-all-start.1 = ((f32[32,1,1280]{2,1,0:T(1,128)}), f32[32,1,1280]{2,1,0:T(1,128)S(1)}, u32[]{:S(2)}, u32[]{:S(2)}) async-start(f32[32,1,1280]{2,1,0:T(1,128)} %reshape.213), calls=%async_computation.2 | async-start | bytes 327680 | tf_op jit(solution)/shard_map/all_to_all | solution.py:52
  202.4 9.2 %collective-permute-start.7 = (f32[4,18,1,256]{3,0,2,1:T(4,128)S(1)}, f32[4,18,1,256]{3,0,2,1:T(4,128)S(1)}, u32[]{:S(2)}, u32[]{:S(2)}) collective-permute-start(f32[4,18,1,256]{3,0,2,1:T(4,128)S(1)} %copy.875), channel_id=1, source_target_pairs={{0,2},{2,4},{4,6},{6,8},{8,10},{10,12},{12,14},{14,0},{1,3},{3,5},... | collective-permute-start | bytes 221192 | tf_op jit(solution)/shard_map/ppermute | solution.py:29
  207.2 7.5 %collective-permute-start.8 = (f32[4,18,1,256]{3,0,2,1:T(4,128)S(1)}, f32[4,18,1,256]{3,0,2,1:T(4,128)S(1)}, u32[]{:S(2)}, u32[]{:S(2)}) collective-permute-start(f32[4,18,1,256]{3,0,2,1:T(4,128)S(1)} %copy.876), channel_id=1, source_target_pairs={{2,0},{4,2},{6,4},{8,6},{10,8},{12,10},{14,12},{0,14},{3,1},{5,3},... | collective-permute-start | bytes 221192 | tf_op jit(solution)/shard_map/ppermute | solution.py:31
  (8 other events, 17.0 us)
Sparse Core Ops, SparseCore 0:
  24.7 37.1 reduce-scatter.1
